TPU v7x, 128 devices: a whole 4x4x4 slice. The times are simulated.
128 devices in a mesh: row: 16 (over y_lo, z, core), col: 8 (over x, y_hi).
Axes of the slice: x: 4, y: 4 (y_hi: 2, y_lo: 2; y = y_hi * 2 + y_lo), z: 4, core: 2. Of those that a mesh axis runs over, the one named last changes fastest.
Arguments:
- hidden_in: bfloat16 [8192, 2048], P('row'), may hold values from -6 to 6
- gain_attn: float32 [2048], replicated, may hold values from 0.1 to 1.9
- gain_mlp: float32 [2048], replicated, may hold values from 0.1 to 1.9
- w_qkv: bfloat16 [2048, 3, 2048], P('row', None, 'col'), may hold values from -0.25 to 0.25
- w_up: bfloat16 [2048, 8192], P('row', 'col'), may hold values from -0.25 to 0.25
- w_out: bfloat16 [2048, 2048], P('col', 'row'), may hold values from -0.125 to 0.125
- w_down: bfloat16 [8192, 2048], P('col', 'row'), may hold values from -0.0625 to 0.0625
- prefix_cache: bfloat16 [128, 128, 2, 2048], P('row', None, None, 'col'), may hold values from -136 to 136, as said below
- suffix_lengths: int32 [64], replicated, may hold values from 1 to 512, 8192 in all
- cached_lengths: int32 [64], replicated, may hold values from 1 to 8192, as said below
- request_group: int32 [64], replicated, may hold values from 0 to 1
- page_table: int32 [128], replicated, may hold values from 0 to 127, each once
Outputs:
- hidden_out: bfloat16 [8192, 2048], P('row', 'col')
- suffix_keys: bfloat16 [8192, 2048], P('row', 'col')
- suffix_values: bfloat16 [8192, 2048], P('row', 'col')
Inputs may be any that keep to these rules, and one draw needn't show every extreme that they name: `suffix_lengths`: the lengths sum to 8192; some request has exactly 512 tokens. `cached_lengths`: some request reuses all 8192 tokens of its prefix. `page_table`: each slot appears once; slot s is held by index s // 8 of row. `prefix_cache`: keys and values of the prefix pages.
All inputs are finite; a program needn't handle non-finite values.
Results may differ from a plain program's by a relative error of at most 0.02.
Values may be sent and summed in bfloat16 or wider, within the bound.
A program may use at most 128 MiB of HBM per device.

v0:
```python
import math
import jax
import jax.numpy as jnp
from jax import lax
from jax.sharding import PartitionSpec as P

HD = 256
ROT = 64
PAGE = 128
GROUPS = 2
very_low = -1e30
norm_epsilon = 1e-05


def from_behind(block, axis, distance):
    devices = range(lax.axis_size(axis))
    route = [(i - distance, i) for i in devices if i - distance in devices]
    return lax.ppermute(block, axis, route)


def layer_normalize(values):
    floats = values.astype(jnp.float32)
    average = jnp.mean(floats, -1, keepdims=True)
    centered = floats - average
    spread = jnp.mean(centered * centered, -1, keepdims=True)
    return centered * lax.rsqrt(spread + norm_epsilon)


def rotary(vectors, position):
    half_rot = ROT // 2
    exponent = jnp.arange(half_rot, dtype=jnp.float32) * (2.0 / ROT)
    frequency = 10000.0 ** (-exponent)
    angles = position.astype(jnp.float32)[:, None] * frequency[None, :]
    cosine = jnp.concatenate([jnp.cos(angles), jnp.cos(angles)], 1)[:, None, :]
    sine = jnp.concatenate([jnp.sin(angles), jnp.sin(angles)], 1)[:, None, :]
    rotated = vectors[..., :ROT]
    turned = jnp.concatenate([-rotated[..., half_rot:], rotated[..., :half_rot]], -1)
    return jnp.concatenate([rotated * cosine + turned * sine, vectors[..., ROT:]], -1)


def token_table(suffix_lengths, cached_lengths, request_group, count):
    starts = jnp.cumsum(suffix_lengths, dtype=jnp.int32) - suffix_lengths
    token_ids = jnp.arange(count, dtype=jnp.int32)
    request = (
        jnp.sum((starts[None, :] <= token_ids[:, None]).astype(jnp.int32), 1, dtype=jnp.int32) - 1
    )
    onehot = (
        request[:, None] == jnp.arange(suffix_lengths.shape[0], dtype=jnp.int32)[None, :]
    ).astype(jnp.int32)
    begin = jnp.sum(onehot * starts[None, :], 1, dtype=jnp.int32)
    limit = jnp.sum(onehot * cached_lengths[None, :], 1, dtype=jnp.int32)
    group_of = jnp.sum(onehot * request_group[None, :], 1, dtype=jnp.int32)
    return (request, limit + token_ids - begin, group_of, limit)


def partial_softmax(scores, visible, value_block):
    allowed = visible[None, :, :]
    peak = jnp.max(jnp.where(allowed, scores, very_low), -1)
    weights = jnp.where(allowed, jnp.exp(scores - peak[..., None]), 0.0)
    total = jnp.sum(weights, -1)
    mixed = jnp.einsum(
        "hqk,khe->qhe",
        weights.astype(jnp.bfloat16),
        value_block,
        preferred_element_type=jnp.float32,
    )
    return (peak, total, mixed)


def combine(earlier, later):
    peak = jnp.maximum(earlier[0], later[0])
    scale_one = jnp.exp(earlier[0] - peak)
    scale_two = jnp.exp(later[0] - peak)
    total = earlier[1] * scale_one + later[1] * scale_two
    mixed = earlier[2] * scale_one.T[:, :, None] + later[2] * scale_two.T[:, :, None]
    return (peak, total, mixed)


def prefix_fold(running, cache_rows, query_block, query_group, query_limit, page_table):
    count = cache_rows.shape[0]
    stride = math.gcd(count, 8)
    heads_here = query_block.shape[1]
    per_prefix = page_table.shape[0] // GROUPS
    table_index = jnp.arange(page_table.shape[0], dtype=jnp.int32)

    def advance(turn_index, inner):
        block_rows = lax.dynamic_slice_in_dim(cache_rows, turn_index * stride, stride, 0)
        slots = turn_index * stride + jnp.arange(stride, dtype=jnp.int32)
        logical = jnp.sum(
            table_index[None, :] * (page_table[None, :] == slots[:, None]).astype(jnp.int32),
            1,
            dtype=jnp.int32,
        )
        key_group = jnp.repeat(logical // per_prefix, PAGE)
        key_position = (
            (logical % per_prefix)[:, None] * PAGE + jnp.arange(PAGE, dtype=jnp.int32)[None, :]
        ).reshape(-1)
        key_block = block_rows[:, :, 0].reshape(stride * PAGE, heads_here, HD)
        value_block = block_rows[:, :, 1].reshape(stride * PAGE, heads_here, HD)
        visible = (key_group[None, :] == query_group[:, None]) & (
            key_position[None, :] < query_limit[:, None]
        )
        scores = jnp.einsum(
            "qhe,khe->hqk", query_block, key_block, preferred_element_type=jnp.float32
        )
        return combine(inner, partial_softmax(scores, visible, value_block))

    return lax.fori_loop(0, count // stride, advance, running)


def body(
    hidden_in,
    gain_attn,
    gain_mlp,
    w_qkv,
    w_up,
    w_out,
    w_down,
    prefix_cache,
    suffix_lengths,
    cached_lengths,
    request_group,
    page_table,
):
    row_count = hidden_in.shape[0]
    model_width = hidden_in.shape[1]
    row_total = lax.axis_size("row")
    col_total = lax.axis_size("col")
    row_place = lax.axis_index("row")
    col_place = lax.axis_index("col")
    head_width = w_qkv.shape[2]
    heads_here = head_width // HD
    normed = layer_normalize(hidden_in)
    attn_in = (normed * gain_attn).astype(jnp.bfloat16)
    mlp_in = (normed * gain_mlp).astype(jnp.bfloat16)
    rows_here = w_qkv.shape[0]
    qkv_columns = 3 * head_width
    joined = jnp.concatenate([w_qkv.reshape(rows_here, qkv_columns), w_up], 1)
    joined = lax.all_gather(joined, "row", axis=0, tiled=True)
    qkv_all = joined[:, :qkv_columns].reshape(model_width, 3, head_width)
    projected = jnp.einsum("td,dkh->tkh", attn_in, qkv_all, preferred_element_type=jnp.float32)
    up_sum = jnp.dot(mlp_in, joined[:, qkv_columns:], preferred_element_type=jnp.float32)
    token_total = row_total * row_count
    request_all, position_all, group_all, limit_all = token_table(
        suffix_lengths, cached_lengths, request_group, token_total
    )
    first_row = row_place * row_count
    local_request = lax.dynamic_slice_in_dim(request_all, first_row, row_count, 0)
    local_position = lax.dynamic_slice_in_dim(position_all, first_row, row_count, 0)
    local_group = lax.dynamic_slice_in_dim(group_all, first_row, row_count, 0)
    local_limit = lax.dynamic_slice_in_dim(limit_all, first_row, row_count, 0)
    projected = projected.reshape(row_count, 3, heads_here, HD)
    queries = (rotary(projected[:, 0], local_position) * HD ** (-0.5)).astype(jnp.bfloat16)
    keys_flat = (
        rotary(projected[:, 1], local_position).astype(jnp.bfloat16).reshape(row_count, head_width)
    )
    values_flat = projected[:, 2].astype(jnp.bfloat16).reshape(row_count, head_width)
    pair_rows = jnp.stack([keys_flat, values_flat], 1)
    previous = from_behind(pair_rows, "row", 1)
    window = jnp.concatenate([previous, pair_rows], 0)
    window_ids = first_row - row_count + jnp.arange(2 * row_count, dtype=jnp.int32)
    padded_request = jnp.concatenate([jnp.full((row_count,), -1, jnp.int32), request_all], 0)
    window_request = lax.dynamic_slice_in_dim(padded_request, first_row, 2 * row_count, 0)
    token_ids = first_row + jnp.arange(row_count, dtype=jnp.int32)
    visible = (window_request[None, :] == local_request[:, None]) & (
        window_ids[None, :] <= token_ids[:, None]
    )
    window_keys = window[:, 0].reshape(2 * row_count, heads_here, HD)
    window_values = window[:, 1].reshape(2 * row_count, heads_here, HD)
    scores = jnp.einsum("qhe,khe->hqk", queries, window_keys, preferred_element_type=jnp.float32)
    suffix_state = partial_softmax(scores, visible, window_values)
    start_state = (
        jnp.full((heads_here, row_count), very_low, jnp.float32),
        jnp.zeros((heads_here, row_count), jnp.float32),
        jnp.zeros((row_count, heads_here, HD), jnp.float32),
    )
    prefix_state = prefix_fold(
        start_state,
        lax.all_gather(prefix_cache, "row", axis=0, tiled=True),
        queries,
        local_group,
        local_limit,
        page_table,
    )
    final = combine(prefix_state, suffix_state)
    attention = (
        (final[2] / final[1].T[:, :, None]).astype(jnp.bfloat16).reshape(row_count, head_width)
    )
    activated = jax.nn.gelu(up_sum, approximate=False).astype(jnp.bfloat16)
    out_rows = w_out.shape[0]
    joined = jnp.concatenate([w_out.T, w_down.T], 1)
    joined = lax.all_gather(joined, "row", axis=0, tiled=True)
    contribution = jnp.einsum(
        "th,dh->td", attention, joined[:, :out_rows], preferred_element_type=jnp.float32
    ) + jnp.einsum("tf,df->td", activated, joined[:, out_rows:], preferred_element_type=jnp.float32)
    summed = lax.psum_scatter(
        contribution.astype(jnp.bfloat16), "col", scatter_dimension=1, tiled=True
    ).astype(jnp.float32)
    share = model_width // col_total
    residual = lax.dynamic_slice_in_dim(hidden_in, col_place * share, share, 1).astype(jnp.float32)
    return ((residual + summed).astype(jnp.bfloat16), keys_flat, values_flat)


def solution(mesh):
    in_specs = (
        P("row", None),
        P(),
        P(),
        P("row", None, "col"),
        P("row", "col"),
        P("col", "row"),
        P("col", "row"),
        P("row", None, None, "col"),
        P(),
        P(),
        P(),
        P(),
    )
    out_specs = (P("row", "col"), P("row", "col"), P("row", "col"))
    return jax.shard_map(body, mesh=mesh, in_specs=in_specs, out_specs=out_specs, check_vma=False)
```

profile of v0, /device:TPU:0, one launch (start us, length us, event | category | flops | bytes accessed | tf_op | source)
XLA Modules:
  0.0 390.6 jit_solution(15160892057513650524)
XLA Ops:
  8.6 1.8 pad_maximum_fusion.1
  15.8 44.4 %all-gather.6.cloned.1.call-done = bf16[2048,1792]{1,0:T(8,128)(2,1)} async-done(((bf16[128,1792]{1,0:T(8,128)(2,1)}), bf16[2048,1792]{1,0:T(8,128)(2,1)}) %all-gather.6.cloned.1.call-update) | async-done | bytes 7340048 | tf_op jit(solution)/shard_map/all_gather | solution.py:139
  60.2 1.9 slice-done
  62.1 3.0 copy.37
  65.1 4.5 %fusion.40 = f32[512,3,256]{0,2,1:T(8,128)S(1)} fusion(bf16[2048,3,256]{0,2,1:T(8,128)(2,1)} %bitcast.156, bf16[512,2048]{1,0:T(8,128)(2,1)} %param.14, f32[2048]{0:T(1024)S(1)} %copy-done.15, f32[512]{0:T(512)S(1)} %add_rsqrt_fusion, f32[512]{0:T(512)S(1)} %broadcast_multiply_fusion), kind=kOutput, calls=%fused_computation.61 | convolution fusion | flops 1615855616 | bytes 6828032 | tf_op jit(solution)/shard_map/td,dkh->tkh/dot_general | solution.py:141
  72.1 3.0 collective-permute-start
  75.0 39.2 %all-gather.8.cloned.1.call-done = bf16[2048,1280]{0,1:T(8,128)(2,1)} async-done(((bf16[128,1280]{0,1:T(8,128)(2,1)}), bf16[2048,1280]{0,1:T(8,128)(2,1)}) %all-gather.8.cloned.1.call-update) | async-done | bytes 5242896 | tf_op jit(solution)/shard_map/all_gather | solution.py:192
  114.3 14.3 %fusion.31 = f32[512,2048]{1,0:T(8,128)} fusion(bf16[2048,1280]{0,1:T(8,128)(2,1)} %all-gather.8.cloned.1.call-done, bf16[2048,1792]{1,0:T(8,128)(2,1)} %all-gather.6.cloned.1.call-done, bf16[512,2048]{1,0:T(8,128)(2,1)S(1)} %copy-done.1, f32[2048]{0:T(1024)S(1)} %copy-done.16, f32[512]{0:T(512)S(1)} %add_rsqrt_fusion, f32[512]{0:T(512)S(1)} %broadcast_multiply_fusion), kind=kOutput, calls=%fused_computation.51 | convolution fusion | flops 4334288896 | bytes 14692352 | tf_op jit(solution)/shard_map/tf,df->td/dot_general | solution.py:195
  132.7 1.3 copy-done.2
  134.8 73.3 %all-gather.4.cloned.1.call-done = bf16[128,128,2,256]{3,1,0,2:T(8,128)(2,1)} async-done(((bf16[8,128,2,256]{3,1,0,2:T(8,128)(2,1)}), bf16[128,128,2,256]{3,1,0,2:T(8,128)(2,1)}) %all-gather.4.cloned.1.call-update) | async-done | bytes 16777232 | tf_op jit(solution)/shard_map/all_gather | solution.py:179
  208.1 91.4 %while.20 = (s32[]{:T(128)}, f32[1,512]{1,0:T(1,128)S(1)}, f32[1,512]{1,0:T(1,128)S(1)}, f32[512,1,256]{0,2,1:T(8,128)}, s32[128]{0:T(128)S(1)}, /*index=5*/s32[...) while((s32[]{:T(128)}, f32[1,512]{1,0:T(1,128)S(1)}, ...), condition=%wide.region_11.12_spmd.clone, body=%wide.region_7.0_spmd.clone.sunk | while | flops 546315392 | bytes 11871218 | solution.py:108
  208.1 1.3 constant_dynamic-slice_fusion.3
  211.1 1.7 fusion.186
  212.8 1.3 constant_dynamic-slice_fusion.3
  215.9 2.7 fusion.186
  221.6 2.7 fusion.186
  227.4 2.7 fusion.186
  233.2 2.7 fusion.186
  239.0 2.7 fusion.186
  244.7 2.7 fusion.186
  250.5 2.7 fusion.186
  256.3 2.7 fusion.186
  262.1 2.7 fusion.186
  267.8 2.7 fusion.186
  273.6 2.7 fusion.186
  279.4 2.7 fusion.186
  285.2 2.7 fusion.186
  290.9 2.7 fusion.186
  296.7 2.7 fusion.186
  299.5 6.3 %add_convert_fusion = bf16[512,2048]{1,0:T(8,128)(2,1)} fusion(f32[512,2048]{1,0:T(8,128)} %fusion.31, bf16[2048,1280]{0,1:T(8,128)(2,1)} %all-gather.8.cloned.1.call-done, f32[512,1024]{1,0:T(8,128)} %copy-done.2, f32[512]{0:T(512)S(1)} %get-tuple-element.373, s32[1024]{0:T(1024)S(1)} %get-tuple-element.378, s32[1024]{0:T(1024)S(1)} %get-tuple-element.377, ...), kind=kOutput, calls=%fused_computation.55 | convolution fusion | flops 811204608 | bytes 10506240 | tf_op jit(solution)/shard_map/th,dh->td/dot_general | solution.py:193
  307.5 74.7 %reduce-scatter.2.cloned.1.call-done = bf16[512,256]{1,0:T(8,128)(2,1)} async-done(((bf16[512,2048]{1,0:T(8,128)(2,1)}), bf16[512,256]{1,0:T(8,128)(2,1)}) %reduce-scatter.2.cloned.1.call-update) | async-done | bytes 262160 | tf_op jit(solution)/shard_map/reduce_scatter | solution.py:196
  382.3 1.8 add_convert_fusion.1
  (243 shorter events, 61.6 us)
Async XLA Ops:
  7.2 3.3 copy-start.11
  7.2 3.3 copy-start.9
  7.2 4.1 %copy-start.6 = (bf16[8,128,2,256]{3,2,1,0:T(2,128)(2,1)S(1)}, bf16[8,128,2,256]{3,2,1,0:T(2,128)(2,1)}, u32[]{:S(2)}) copy-start(bf16[8,128,2,256]{3,2,1,0:T(2,128)(2,1)} %param.21) | copy-start | bytes 3145732
  7.2 53.0 %all-gather.6.cloned.1.call-start = ((), (), s32[]{:S(2)}) async-start(), calls=%async_computation.2 | async-start | bytes 7798784 | tf_op jit(solution)/shard_map/all_gather | solution.py:139
  10.4 2.2 copy-start.12
  10.4 103.9 %all-gather.8.cloned.1.call-start = ((), (), s32[]{:S(2)}) async-start(), calls=%async_computation.3 | async-start | bytes 5570560 | tf_op jit(solution)/shard_map/all_gather | solution.py:192
  10.5 2.9 copy-start.13
  10.5 2.9 copy-start.14
  11.2 3.2 copy-start
  11.3 196.8 %all-gather.4.cloned.1.call-start = ((), (), s32[]{:S(2)}) async-start(), calls=%async_computation.1 | async-start | bytes 17825792 | tf_op jit(solution)/shard_map/all_gather | solution.py:179
  12.5 369.8 %reduce-scatter.2.cloned.1.call-start = ((), (), s32[]{:S(2)}) async-start(), calls=%async_computation.4 | async-start | bytes 2359296 | tf_op jit(solution)/shard_map/reduce_scatter | solution.py:196
  60.2 1.9 slice-start
  62.1 3.0 copy-start.15
  69.7 44.6 %copy-start.1 = (bf16[512,2048]{1,0:T(8,128)(2,1)S(1)}, bf16[512,2048]{1,0:T(8,128)(2,1)}, u32[]{:S(2)}) copy-start(bf16[512,2048]{1,0:T(8,128)(2,1)} %param.14) | copy-start | bytes 6291460
  69.7 44.5 %copy-start.16 = (f32[2048]{0:T(1024)S(1)}, f32[2048]{0:T(1024)}, u32[]{:S(2)}) copy-start(f32[2048]{0:T(1024)} %param.16) | copy-start | bytes 24580
  72.1 58.4 %collective-permute-start = (bf16[512,2,256]{0,2,1:T(8,128)(2,1)}, bf16[512,2,256]{0,2,1:T(8,128)(2,1)}, u32[]{:S(2)}, u32[]{:S(2)}) collective-permute-start(bf16[512,2,256]{0,2,1:T(8,128)(2,1)} %pad_maximum_fusion), channel_id=1, source_target_pairs={{0,8},{8,16},{16,24},{24,32},{32,40},{40,48},{48,56},{56,64},{64,7... | collective-permute-start | bytes 1572872 | tf_op jit(solution)/shard_map/ppermute | solution.py:18
  128.6 1.9 copy-start.4
  128.6 3.1 copy-start.8
  132.7 75.4 %copy-start.17 = (s32[128]{0:T(128)S(1)}, s32[128]{0:T(128)}, u32[]{:S(2)}) copy-start(s32[128]{0:T(128)} %param.25) | copy-start | bytes 1540
  208.1 1.6 copy-start.10
  212.8 1.6 copy-start.10
  218.6 1.6 copy-start.10
  224.3 1.6 copy-start.10
  230.1 1.6 copy-start.10
  235.9 1.6 copy-start.10
  241.7 1.6 copy-start.10
  247.5 1.6 copy-start.10
  253.2 1.6 copy-start.10
  259.0 1.6 copy-start.10
  276.3 1.6 copy-start.10
  282.1 1.6 copy-start.10
  287.9 1.6 copy-start.10
  (7 other events, 9.6 us)
Sparse Core Ops, SparseCore 0:
  10.5 49.6 all-gather.5
  61.8 52.3 all-gather.7
  115.9 92.0 all-gather.3
  305.9 76.3 reduce-scatter.1
where the time goes:
time: 392 us; the launch traced here: 391 us
  waiting for transfers between devices  232 us (59%)
  matrix products  77.4 us (20%)
  local copies, waits for them, and re-layouts  33.8 us (9%)
  other arithmetic  30.1 us (8%)
  between operations  14 us (4%)
    all_gather x2, waiting for transfers between devices, body(): joined = lax.all_gather(joined, 'row', axis=0, tiled=True)  83.6 us
    reduce_scatter x1, waiting for transfers between devices, body(): lax.psum_scatter(contribution.astype(jnp.bfloat16), 'col', scatter_dimens...  74.7 us
    all_gather x1, waiting for transfers between devices, body(): lax.all_gather(prefix_cache, 'row', axis=0, tiled=True)  73.3 us
    dot_general x16, matrix products, partial_softmax(): jnp.einsum('hqk,khe->qhe', weights.astype(jnp.bfloat16), value_block, pre...  42.5 us
    slice x16, local copies, waits for them, and re-layouts, advance(): value_block = block_rows[:, :, 1].reshape(stride * PAGE, heads_here, HD)  21 us
    dot_general x1, matrix products, body(): jnp.einsum('tf,df->td', activated, joined[:, out_rows:], preferred_elemen...  14.3 us
    reduce_sum x17, other arithmetic, partial_softmax(): total = jnp.sum(weights, -1)  14.2 us
    dot_general x16, matrix products, advance(): jnp.einsum('qhe,khe->hqk', query_block, key_block, preferred_element_type...  9.17 us
  transfers between devices with their start and end apart: 5, of which 4 were waited for; matrix products, arithmetic and copies ran while one was open for 9% of the time, Pallas kernels for 0%

commit v1 on v0

--- a/solution.py
+++ b/solution.py
@@ -176,7 +176,9 @@
     )
     prefix_state = prefix_fold(
         start_state,
-        lax.all_gather(prefix_cache, "row", axis=0, tiled=True),
+        jnp.concatenate(
+            lax.all_to_all(jnp.stack([prefix_cache] * lax.axis_size("row")), "row", 0, 0), axis=0
+        ),
         queries,
         local_group,
         local_limit,

time: 392 us -> 519 us (1.32)
  waiting for transfers between devices: 232 us -> 333 us
  local copies, waits for them, and re-layouts: 33.8 us -> 53 us
  starting transfers between devices: 3.13 us -> 9.79 us
    all_gather x2, waiting for transfers between devices: 83.6 us -> 260 us  [body(): joined = lax.all_gather(joined, 'row', axis=0, tiled=True)]
    all_gather x1 -> x0, waiting for transfers between devices: 73.3 us -> none  [body(): lax.all_gather(prefix_cache, 'row', axis=0, tiled=True)]
    all_to_all x0 -> x1, local copies, waits for them, and re-layouts: none -> 14.2 us  [body(): lax.all_to_all(jnp.stack([prefix_cache] * lax.axis_size('row')), 'row', 0...]
    all_to_all x0 -> x1, starting transfers between devices: none -> 6.71 us  [body(): lax.all_to_all(jnp.stack([prefix_cache] * lax.axis_size('row')), 'row', 0...]
    another operation x1 -> x2, local copies, waits for them, and re-layouts: 0.1 us -> 6.04 us  [the longest x1 5.94 us: body(): jnp.stack([prefix_cache] * lax.axis_size('row'))]
  transfers between devices with their start and end apart: 5 -> 5, of which waited for: 4 -> 3; matrix products, arithmetic and copies ran while one was open for 9% -> 8% of each run, Pallas kernels for 0% -> 0%
where the time goes in v1:
time: 519 us; the launch traced here: 518 us
  waiting for transfers between devices  333 us (64%)
  matrix products  77.2 us (15%)
  local copies, waits for them, and re-layouts  53 us (10%)
  other arithmetic  30 us (6%)
  between operations  14.1 us (3%)
  starting transfers between devices  9.79 us (2%)
    all_gather x2, waiting for transfers between devices, body(): joined = lax.all_gather(joined, 'row', axis=0, tiled=True)  260 us
    reduce_scatter x1, waiting for transfers between devices, body(): lax.psum_scatter(contribution.astype(jnp.bfloat16), 'col', scatter_dimens...  73.7 us
    dot_general x16, matrix products, partial_softmax(): jnp.einsum('hqk,khe->qhe', weights.astype(jnp.bfloat16), value_block, pre...  42.2 us
    slice x16, local copies, waits for them, and re-layouts, advance(): value_block = block_rows[:, :, 1].reshape(stride * PAGE, heads_here, HD)  21 us
    dot_general x1, matrix products, body(): jnp.einsum('tf,df->td', activated, joined[:, out_rows:], preferred_elemen...  14.3 us
    reduce_sum x17, other arithmetic, partial_softmax(): total = jnp.sum(weights, -1)  14.2 us
    all_to_all x1, local copies, waits for them, and re-layouts, body(): lax.all_to_all(jnp.stack([prefix_cache] * lax.axis_size('row')), 'row', 0...  14.2 us
  transfers between devices with their start and end apart: 5, of which 3 were waited for; matrix products, arithmetic and copies ran while one was open for 8% of the time, Pallas kernels for 0%

profile of v1, /device:TPU:0, one launch (start us, length us, event | category | flops | bytes accessed | tf_op | source)
XLA Modules:
  0.0 517.7 jit_solution(10592641433756815120)
XLA Ops:
  8.5 1.8 pad_maximum_fusion.1
  10.5 5.9 %stack.4 = bf16[16,8,128,2,256]{4,2,1,3,0:T(8,128)(2,1)} broadcast(bf16[8,128,2,256]{3,1,0,2:T(8,128)(2,1)S(1)} %copy.56), dimensions={1,2,3,4} | broadcast | bytes 17825792 | tf_op jit(solution)/shard_map/stack | solution.py:180
  16.5 6.7 %all-to-all-start = ((bf16[16,8,128,2,256]{4,2,1,3,0:T(8,128)(2,1)}), bf16[16,8,128,2,256]{4,2,1,3,0:T(8,128)(2,1)}, u32[]{:S(2)}, u32[]{:S(2)}) async-start(bf16[16,8,128,2,256]{4,2,1,3,0:T(8,128)(2,1)} %stack.4), calls=%async_computation | async-start | bytes 33554432 | tf_op jit(solution)/shard_map/all_to_all | solution.py:180
  27.4 212.1 %all-gather.3.cloned.1.call-done = bf16[2048,1792]{1,0:T(8,128)(2,1)} async-done(((bf16[128,1792]{1,0:T(8,128)(2,1)}), bf16[2048,1792]{1,0:T(8,128)(2,1)}) %all-gather.3.cloned.1.call-update) | async-done | bytes 7340048 | tf_op jit(solution)/shard_map/all_gather | solution.py:139
  239.4 1.9 slice-done
  241.3 3.0 copy.60
  244.3 4.5 fusion.40
  251.2 3.0 collective-permute-start
  254.2 47.4 %all-gather.5.cloned.1.call-done = bf16[2048,1280]{0,1:T(8,128)(2,1)} async-done(((bf16[128,1280]{0,1:T(8,128)(2,1)}), bf16[2048,1280]{0,1:T(8,128)(2,1)}) %all-gather.5.cloned.1.call-update) | async-done | bytes 5242896 | tf_op jit(solution)/shard_map/all_gather | solution.py:194
  301.7 14.3 %fusion.31 = f32[512,2048]{1,0:T(8,128)} fusion(bf16[2048,1280]{0,1:T(8,128)(2,1)} %all-gather.5.cloned.1.call-done, bf16[2048,1792]{1,0:T(8,128)(2,1)} %all-gather.3.cloned.1.call-done, bf16[512,2048]{1,0:T(8,128)(2,1)S(1)} %copy-done.1, f32[2048]{0:T(1024)S(1)} %copy-done.16, f32[512]{0:T(512)S(1)} %add_rsqrt_fusion, f32[512]{0:T(512)S(1)} %broadcast_multiply_fusion), kind=kOutput, calls=%fused_computation.51 | convolution fusion | flops 4334288896 | bytes 14692352 | tf_op jit(solution)/shard_map/tf,df->td/dot_general | solution.py:197
  320.1 1.3 copy-done.2
  322.2 14.2 %copy.57 = bf16[16,8,128,2,256]{4,2,3,1,0:T(8,128)(2,1)} copy(bf16[16,8,128,2,256]{4,2,1,3,0:T(8,128)(2,1)} %all-to-all-done) | data formatting | bytes 33554432 | tf_op jit(solution)/shard_map/all_to_all | solution.py:180
  336.4 91.1 %while.20 = (s32[]{:T(128)}, f32[1,512]{1,0:T(1,128)S(1)}, f32[1,512]{1,0:T(1,128)S(1)}, f32[512,1,256]{0,2,1:T(8,128)}, s32[128]{0:T(128)S(1)}, /*index=5*/s32[...) while((s32[]{:T(128)}, f32[1,512]{1,0:T(1,128)S(1)}, ...), condition=%wide.region_11.12_spmd.clone, body=%wide.region_7.0_spmd.clone.sunk | while | flops 546315392 | bytes 11871218 | solution.py:108
  339.5 1.7 fusion.186
  344.2 2.7 fusion.186
  350.0 2.7 fusion.186
  355.7 2.7 fusion.186
  361.5 2.7 fusion.186
  367.2 2.7 fusion.186
  373.0 2.7 fusion.186
  378.8 2.7 fusion.186
  384.5 2.7 fusion.186
  390.3 2.7 fusion.186
  396.0 2.7 fusion.186
  401.8 2.7 fusion.186
  407.6 2.7 fusion.186
  413.3 2.7 fusion.186
  419.1 2.7 fusion.186
  424.8 2.7 fusion.186
  427.6 6.3 %add_convert_fusion = bf16[512,2048]{1,0:T(8,128)(2,1)} fusion(f32[512,2048]{1,0:T(8,128)} %fusion.31, bf16[2048,1280]{0,1:T(8,128)(2,1)} %all-gather.5.cloned.1.call-done, f32[512,1024]{1,0:T(8,128)} %copy-done.2, f32[512]{0:T(512)S(1)} %get-tuple-element.397, s32[1024]{0:T(1024)S(1)} %get-tuple-element.402, s32[1024]{0:T(1024)S(1)} %get-tuple-element.401, ...), kind=kOutput, calls=%fused_computation.55 | convolution fusion | flops 811204608 | bytes 10506240 | tf_op jit(solution)/shard_map/th,dh->td/dot_general | solution.py:195
  435.7 73.7 %reduce-scatter.2.cloned.1.call-done = bf16[512,256]{1,0:T(8,128)(2,1)} async-done(((bf16[512,2048]{1,0:T(8,128)(2,1)}), bf16[512,256]{1,0:T(8,128)(2,1)}) %reduce-scatter.2.cloned.1.call-update) | async-done | bytes 262160 | tf_op jit(solution)/shard_map/reduce_scatter | solution.py:198
  509.4 1.8 add_convert_fusion.1
  (244 shorter events, 63.2 us)
Async XLA Ops:
  7.2 3.2 copy-start.6
  7.2 232.2 %all-gather.3.cloned.1.call-start = ((), (), s32[]{:S(2)}) async-start(), calls=%async_computation.2 | async-start | bytes 7798784 | tf_op jit(solution)/shard_map/all_gather | solution.py:139
  16.4 6.8 %copy-start.9 = (bf16[1024,128]{1,0:T(8,128)(2,1)S(1)}, bf16[1024,128]{1,0:T(8,128)(2,1)}, u32[]{:S(2)}) copy-start(bf16[1024,128]{1,0:T(8,128)(2,1)} %param.20) | copy-start | bytes 786436
  16.4 6.8 %copy-start.11 = (bf16[256,128]{1,0:T(8,128)(2,1)S(1)}, bf16[256,128]{1,0:T(8,128)(2,1)}, u32[]{:S(2)}) copy-start(bf16[256,128]{1,0:T(8,128)(2,1)} %param.19) | copy-start | bytes 196612
  16.5 7.7 %copy-start.12 = (s32[64]{0:T(128)S(1)}, s32[64]{0:T(128)}, u32[]{:S(2)}) copy-start(s32[64]{0:T(128)} %param.22) | copy-start | bytes 772
  16.5 8.5 %copy-start.13 = (s32[64]{0:T(128)S(1)}, s32[64]{0:T(128)}, u32[]{:S(2)}) copy-start(s32[64]{0:T(128)} %param.24) | copy-start | bytes 772
  16.5 8.4 %copy-start.14 = (s32[64]{0:T(128)S(1)}, s32[64]{0:T(128)}, u32[]{:S(2)}) copy-start(s32[64]{0:T(128)} %param.23) | copy-start | bytes 772
  16.5 9.5 %copy-start = (bf16[512,2048]{1,0:T(8,128)(2,1)S(1)}, bf16[512,2048]{1,0:T(8,128)(2,1)}, u32[]{:S(2)}) copy-start(bf16[512,2048]{1,0:T(8,128)(2,1)} %param.14) | copy-start | bytes 6291460
  16.5 305.7 %all-to-all-start = ((bf16[16,8,128,2,256]{4,2,1,3,0:T(8,128)(2,1)}), bf16[16,8,128,2,256]{4,2,1,3,0:T(8,128)(2,1)}, u32[]{:S(2)}, u32[]{:S(2)}) async-start(bf16[16,8,128,2,256]{4,2,1,3,0:T(8,128)(2,1)} %stack.4), calls=%async_computation | async-start | bytes 33554432 | tf_op jit(solution)/shard_map/all_to_all | solution.py:180
  23.2 278.5 %all-gather.5.cloned.1.call-start = ((), (), s32[]{:S(2)}) async-start(), calls=%async_computation.3 | async-start | bytes 5570560 | tf_op jit(solution)/shard_map/all_gather | solution.py:194
  24.0 485.3 %reduce-scatter.2.cloned.1.call-start = ((), (), s32[]{:S(2)}) async-start(), calls=%async_computation.4 | async-start | bytes 2359296 | tf_op jit(solution)/shard_map/reduce_scatter | solution.py:198
  239.4 1.9 slice-start
  241.3 3.0 copy-start.15
  248.9 52.8 %copy-start.1 = (bf16[512,2048]{1,0:T(8,128)(2,1)S(1)}, bf16[512,2048]{1,0:T(8,128)(2,1)}, u32[]{:S(2)}) copy-start(bf16[512,2048]{1,0:T(8,128)(2,1)} %param.14) | copy-start | bytes 6291460
  248.9 52.8 %copy-start.16 = (f32[2048]{0:T(1024)S(1)}, f32[2048]{0:T(1024)}, u32[]{:S(2)}) copy-start(f32[2048]{0:T(1024)} %param.16) | copy-start | bytes 24580
  251.2 66.7 %collective-permute-start = (bf16[512,2,256]{0,2,1:T(8,128)(2,1)}, bf16[512,2,256]{0,2,1:T(8,128)(2,1)}, u32[]{:S(2)}, u32[]{:S(2)}) collective-permute-start(bf16[512,2,256]{0,2,1:T(8,128)(2,1)} %pad_maximum_fusion), channel_id=1, source_target_pairs={{0,8},{8,16},{16,24},{24,32},{32,40},{40,48},{48,56},{56,64},{64,7... | collective-permute-start | bytes 1572872 | tf_op jit(solution)/shard_map/ppermute | solution.py:18
  316.0 1.9 copy-start.4
  316.0 3.1 copy-start.8
  322.2 14.2 %copy-start.17 = (s32[128]{0:T(128)S(1)}, s32[128]{0:T(128)}, u32[]{:S(2)}) copy-start(s32[128]{0:T(128)} %param.25) | copy-start | bytes 1540
  336.4 1.6 copy-start.10
  341.1 1.6 copy-start.10
  346.9 1.6 copy-start.10
  352.7 1.6 copy-start.10
  358.4 1.6 copy-start.10
  364.2 1.6 copy-start.10
  369.9 1.6 copy-start.10
  375.7 1.6 copy-start.10
  381.5 1.6 copy-start.10
  387.2 1.6 copy-start.10
  393.0 1.6 copy-start.10
  398.7 1.6 copy-start.10
  404.5 1.6 copy-start.10
  (7 other events, 9.6 us)
Sparse Core Ops, SparseCore 0:
  10.4 228.9 all-gather.2
  241.0 60.5 all-gather.4
  434.0 75.2 reduce-scatter.1
